TPU v7x, 256 devices: a whole 4x4x8 slice. The times are simulated.
256 devices in a mesh: row: 4 (over y), col: 16 (over z, core), layer: 4 (over x).
Axes of the slice: x: 4, y: 4, z: 8, core: 2. Of those that a mesh axis runs over, the one named last changes fastest.
Arguments:
- blocks: bfloat16 [5632, 128, 128], P(('col', 'layer')), may hold values from -6 to 6
- block_aux: int32 [5632], P(('col', 'layer')), may hold values from 0 to 23
- block_row: int32 [5632], P(('col', 'layer')), may hold values from 0 to 15, as said below
- block_col: int32 [5632], P(('col', 'layer')), may hold values from 0 to 159, as said below
- extents: int32 [5632], P(('col', 'layer')), may hold values from 32 to 128
- occ_green: bfloat16 [20480, 2048], P('layer', 'row'), may hold values from -0.00390625 to 0.00390625
- virt_green: bfloat16 [20480, 2048], P('layer', 'row'), may hold values from -0.00390625 to 0.00390625
Outputs:
- chi: float32 [24, 24], replicated
Inputs may be any that keep to these rules, and one draw needn't show every extreme that they name: block_row[n] numbers the block of 128 window functions that tile n covers. The owner of tile n is the pair (block_row[n], block_col[n] // 40). Within each device's share of 88 consecutive entries no owner appears more than 2 times, and one owner, the same for every share, appears exactly 2 times in every share.
All inputs are finite; a program needn't handle non-finite values.
Results may differ from a plain program's by a relative error of at most 0.0003.
Values may be sent and summed in bfloat16 or wider, within the bound.
No kernel may reach another device: no remote copies, remote signals or barrier semaphores. Data moves between devices by JAX's collectives and lax.ppermute only.
A program may use at most 192 MiB of HBM per device.

v0:
```python
import jax
import jax.numpy as jnp
from jax import lax
from jax.sharding import PartitionSpec as P

NP = 24


def on_device(blocks, block_aux, block_row, block_col, extents, occ_green, virt_green):
    row_count = lax.axis_size("row")
    col_count = lax.axis_size("col")
    layer_count = lax.axis_size("layer")
    held_count = blocks.shape[0]
    tile_side = blocks.shape[1]
    aux_count = NP
    owner_count = col_count * layer_count
    capacity = max(2, held_count // owner_count + 1)
    layer_blocks = occ_green.shape[0] // tile_side
    columns = jnp.arange(tile_side, dtype=jnp.int32)
    masked_tiles = jnp.where(
        columns[None, None, :] < extents[:, None, None], blocks, jnp.zeros((), blocks.dtype)
    )
    layer_of = block_col // layer_blocks
    target = block_row * layer_count + layer_of
    kept_col = block_col - layer_of * layer_blocks
    marked = (target[:, None] == jnp.arange(owner_count, dtype=jnp.int32)[None, :]).astype(
        jnp.int32
    )
    earlier = jnp.cumsum(marked, axis=0) - marked
    placed = target * capacity + jnp.sum(earlier * marked, axis=1)
    send_tiles = (
        jnp.zeros((owner_count * capacity, tile_side, tile_side), blocks.dtype)
        .at[placed]
        .set(masked_tiles)
    )
    send_meta = (
        jnp.zeros((owner_count * capacity, 2), jnp.int32)
        .at[placed]
        .set(jnp.stack([block_aux, kept_col], axis=1))
    )
    send_tiles = send_tiles.reshape(col_count, layer_count, capacity, tile_side, tile_side)
    send_meta = send_meta.reshape(col_count, layer_count, capacity, 2)
    total_slots = col_count * layer_count * capacity
    got_tiles, got_meta = (
        lax.all_to_all(
            send_tiles.reshape(total_slots, tile_side, tile_side),
            ("col", "layer"),
            split_axis=0,
            concat_axis=0,
            tiled=True,
        ),
        lax.all_to_all(
            send_meta.reshape(total_slots, 2),
            ("col", "layer"),
            split_axis=0,
            concat_axis=0,
            tiled=True,
        ),
    )
    group_size = col_count * capacity
    got_tiles = got_tiles.reshape(layer_count, group_size, tile_side, tile_side)
    got_meta = got_meta.reshape(layer_count, group_size, 2)
    occ_cols, virt_cols = (occ_green, virt_green)
    width_here = occ_cols.shape[1]
    offsets = jnp.arange(tile_side, dtype=jnp.int32)

    def add_group(totals, record):
        occ_total, virt_total = totals
        tile_group, meta_group = record
        row_index = meta_group[:, 1][:, None] * tile_side + offsets[None, :]
        occ_rows = occ_cols[row_index]
        virt_rows = virt_cols[row_index]
        occ_term = jnp.einsum(
            "gsv,gls->gvl", occ_rows, tile_group, preferred_element_type=jnp.float32
        )
        virt_term = jnp.einsum(
            "gvs,gsl->gvl", tile_group, virt_rows, preferred_element_type=jnp.float32
        )
        aux_index = meta_group[:, 0]
        return (
            (occ_total.at[aux_index].add(occ_term), virt_total.at[aux_index].add(virt_term)),
            None,
        )

    start_totals = (
        jnp.zeros((aux_count, width_here, tile_side), jnp.float32),
        jnp.zeros((aux_count, tile_side, width_here), jnp.float32),
    )
    (occ_total, virt_total), _ = lax.scan(add_group, start_totals, (got_tiles, got_meta))
    occ_done, virt_done = (
        lax.psum_scatter(occ_total, "layer", scatter_dimension=1, tiled=True),
        lax.psum_scatter(virt_total, "layer", scatter_dimension=2, tiled=True),
    )
    mesh_count = row_count * layer_count
    thin_rows = tile_side // mesh_count
    stack_count = mesh_count // col_count
    narrow = occ_done.shape[1]
    occ_five = occ_done.reshape(aux_count, 1, col_count, thin_rows, tile_side)
    virt_five = virt_done.reshape(aux_count, stack_count, col_count, thin_rows, narrow)
    occ_moved, virt_moved = (
        lax.all_to_all(occ_five, "col", split_axis=2, concat_axis=1, tiled=True),
        lax.all_to_all(virt_five, "col", split_axis=2, concat_axis=1, tiled=True),
    )
    virt_four = virt_moved.reshape(aux_count, mesh_count, thin_rows, narrow)
    virt_back = lax.all_to_all(virt_four, ("row", "layer"), split_axis=1, concat_axis=3, tiled=True)
    occ_final = occ_moved.reshape(aux_count, col_count, thin_rows, tile_side)
    virt_final = virt_back.reshape(aux_count, thin_rows, col_count, tile_side)
    chi_part = jnp.einsum(
        "pcji,qjci->pq",
        occ_final,
        virt_final,
        precision=lax.Precision.HIGHEST,
        preferred_element_type=jnp.float32,
    )
    return lax.psum(chi_part, ("row", "col", "layer"))


def solution(mesh):
    in_specs = (
        P(("col", "layer"), None, None),
        P(("col", "layer")),
        P(("col", "layer")),
        P(("col", "layer")),
        P(("col", "layer")),
        P("layer", "row"),
        P("layer", "row"),
    )
    out_specs = P()
    return jax.shard_map(
        on_device, mesh=mesh, in_specs=in_specs, out_specs=out_specs, check_vma=False
    )
```

profile of v0, /device:TPU:1, one launch (start us, length us, event | category | flops | bytes accessed | tf_op | source)
XLA Modules:
  0.0 813.1 jit_solution(16769600088540931036)
XLA Ops:
  11.0 13.0 %all-to-all-start = ((s32[64,2,2]{1,2,0:T(2,128)}), s32[64,2,2]{1,2,0:T(2,128)S(1)}, u32[]{:S(2)}, u32[]{:S(2)}) async-start(s32[64,2,2]{1,2,0:T(2,128)} %copy.19), calls=%async_computation | async-start | bytes 131072 | tf_op jit(solution)/shard_map/all_to_all | solution.py:52
  29.7 12.7 %scatter_fusion.2 = bf16[128,128,128]{2,1,0:T(8,128)(2,1)} fusion(bf16[128,128,128]{2,1,0:T(8,128)(2,1)} %broadcast_in_dim.41, s32[88]{0:T(128)S(1)} %compare_select_fusion.2, bf16[88,128,128]{2,1,0:T(8,128)(2,1)S(1)} %broadcast_select_fusion), kind=kCustom, calls=%fused_computation.5 | custom fusion | bytes 8651104 | tf_op jit(solution)/shard_map/scatter | solution.py:34
  42.4 10.4 %all-to-all-start.1 = ((bf16[128,128,128]{2,1,0:T(8,128)(2,1)}), bf16[128,128,128]{2,1,0:T(8,128)(2,1)}, u32[]{:S(2)}, u32[]{:S(2)}) async-start(bf16[128,128,128]{2,1,0:T(8,128)(2,1)} %scatter_fusion.2), calls=%async_computation.1 | async-start | bytes 8388608 | tf_op jit(solution)/shard_map/all_to_all | solution.py:45
  53.0 93.4 %all-to-all-done.1 = bf16[128,128,128]{2,1,0:T(8,128)(2,1)} async-done(((bf16[128,128,128]{2,1,0:T(8,128)(2,1)}), bf16[128,128,128]{2,1,0:T(8,128)(2,1)}, u32[]{:S(2)}, u32[]{:S(2)}) %all-to-all-start.1) | async-done | bytes 4194336 | tf_op jit(solution)/shard_map/all_to_all | solution.py:45
  153.2 366.1 %while.13 = (s32[]{:T(128)}, f32[24,512,128]{2,1,0:T(8,128)}, f32[24,128,512]{2,1,0:T(8,128)}, s32[4,32,2]{1,0,2:T(4,128)S(1)}, bf16[5120,512]{1,0:T(8,128)(2,1)...) while((s32[]{:T(128)}, f32[24,512,128]{2,1,0:T(8,128)}, ...), condition=%wide.region_7.8_spmd.clone, body=%wide.region_4.7_spmd.clone.sunk | while | flops 1077956736 | bytes 94423512 | solution.py:89
  153.3 20.6 %gather_fusion.1 = bf16[4096,512]{1,0:T(8,128)(2,1)} fusion(bf16[5120,512]{1,0:T(8,128)(2,1)} %get-tuple-element.167, s32[4096]{0:T(1024)S(1)} %fusion.37), kind=kCustom, calls=%fused_computation.1.clone.clone.1 | custom fusion | bytes 8404992 | tf_op jit(solution)/shard_map/while/body/eval_jaxpr/gather | solution.py:72
  173.8 7.0 fusion.39
  180.8 18.0 %scatter_fusion.1 = f32[24,128,512]{2,1,0:T(8,128)} fusion(f32[24,128,512]{2,1,0:T(8,128)} %get-tuple-element.155, s32[32]{0:T(128)S(1)} %get-tuple-element.143, f32[32,128,512]{2,1,0:T(8,128)} %fusion.39), kind=kCustom, calls=%fused_computation.3.clone.clone.1 | custom fusion | flops 2097152 | bytes 25165952 | tf_op jit(solution)/shard_map/while/body/eval_jaxpr/scatter-add | solution.py:81
  198.8 20.6 %gather_fusion = bf16[4096,512]{1,0:T(8,128)(2,1)} fusion(bf16[5120,512]{1,0:T(8,128)(2,1)} %get-tuple-element.165, s32[4096]{0:T(1024)S(1)} %fusion.37), kind=kCustom, calls=%fused_computation.clone.clone.1 | custom fusion | bytes 8404992 | tf_op jit(solution)/shard_map/while/body/eval_jaxpr/gather | solution.py:71
  219.3 7.0 fusion.38
  226.4 17.8 %scatter_fusion = f32[24,512,128]{2,1,0:T(8,128)} fusion(f32[24,512,128]{2,1,0:T(8,128)} %get-tuple-element.154, s32[32]{0:T(128)S(1)} %get-tuple-element.143, f32[32,512,128]{2,1,0:T(8,128)} %fusion.38), kind=kCustom, calls=%fused_computation.2.clone.clone.1 | custom fusion | flops 2097152 | bytes 25165952 | tf_op jit(solution)/shard_map/while/body/eval_jaxpr/scatter-add | solution.py:81
  244.3 20.6 %gather_fusion.1 = bf16[4096,512]{1,0:T(8,128)(2,1)} fusion(bf16[5120,512]{1,0:T(8,128)(2,1)} %get-tuple-element.167, s32[4096]{0:T(1024)S(1)} %fusion.37), kind=kCustom, calls=%fused_computation.1.clone.clone.1 | custom fusion | bytes 8404992 | tf_op jit(solution)/shard_map/while/body/eval_jaxpr/gather | solution.py:72
  271.8 18.1 %scatter_fusion.1 = f32[24,128,512]{2,1,0:T(8,128)} fusion(f32[24,128,512]{2,1,0:T(8,128)} %get-tuple-element.155, s32[32]{0:T(128)S(1)} %get-tuple-element.143, f32[32,128,512]{2,1,0:T(8,128)} %fusion.39), kind=kCustom, calls=%fused_computation.3.clone.clone.1 | custom fusion | flops 2097152 | bytes 25165952 | tf_op jit(solution)/shard_map/while/body/eval_jaxpr/scatter-add | solution.py:81
  289.9 20.6 %gather_fusion = bf16[4096,512]{1,0:T(8,128)(2,1)} fusion(bf16[5120,512]{1,0:T(8,128)(2,1)} %get-tuple-element.165, s32[4096]{0:T(1024)S(1)} %fusion.37), kind=kCustom, calls=%fused_computation.clone.clone.1 | custom fusion | bytes 8404992 | tf_op jit(solution)/shard_map/while/body/eval_jaxpr/gather | solution.py:71
  310.5 7.0 fusion.38
  317.5 18.1 %scatter_fusion = f32[24,512,128]{2,1,0:T(8,128)} fusion(f32[24,512,128]{2,1,0:T(8,128)} %get-tuple-element.154, s32[32]{0:T(128)S(1)} %get-tuple-element.143, f32[32,512,128]{2,1,0:T(8,128)} %fusion.38), kind=kCustom, calls=%fused_computation.2.clone.clone.1 | custom fusion | flops 2097152 | bytes 25165952 | tf_op jit(solution)/shard_map/while/body/eval_jaxpr/scatter-add | solution.py:81
  335.7 20.6 %gather_fusion.1 = bf16[4096,512]{1,0:T(8,128)(2,1)} fusion(bf16[5120,512]{1,0:T(8,128)(2,1)} %get-tuple-element.167, s32[4096]{0:T(1024)S(1)} %fusion.37), kind=kCustom, calls=%fused_computation.1.clone.clone.1 | custom fusion | bytes 8404992 | tf_op jit(solution)/shard_map/while/body/eval_jaxpr/gather | solution.py:72
  363.3 18.5 %scatter_fusion.1 = f32[24,128,512]{2,1,0:T(8,128)} fusion(f32[24,128,512]{2,1,0:T(8,128)} %get-tuple-element.155, s32[32]{0:T(128)S(1)} %get-tuple-element.143, f32[32,128,512]{2,1,0:T(8,128)} %fusion.39), kind=kCustom, calls=%fused_computation.3.clone.clone.1 | custom fusion | flops 2097152 | bytes 25165952 | tf_op jit(solution)/shard_map/while/body/eval_jaxpr/scatter-add | solution.py:81
  381.7 20.6 %gather_fusion = bf16[4096,512]{1,0:T(8,128)(2,1)} fusion(bf16[5120,512]{1,0:T(8,128)(2,1)} %get-tuple-element.165, s32[4096]{0:T(1024)S(1)} %fusion.37), kind=kCustom, calls=%fused_computation.clone.clone.1 | custom fusion | bytes 8404992 | tf_op jit(solution)/shard_map/while/body/eval_jaxpr/gather | solution.py:71
  402.3 7.0 fusion.38
  409.3 18.4 %scatter_fusion = f32[24,512,128]{2,1,0:T(8,128)} fusion(f32[24,512,128]{2,1,0:T(8,128)} %get-tuple-element.154, s32[32]{0:T(128)S(1)} %get-tuple-element.143, f32[32,512,128]{2,1,0:T(8,128)} %fusion.38), kind=kCustom, calls=%fused_computation.2.clone.clone.1 | custom fusion | flops 2097152 | bytes 25165952 | tf_op jit(solution)/shard_map/while/body/eval_jaxpr/scatter-add | solution.py:81
  427.8 20.6 %gather_fusion.1 = bf16[4096,512]{1,0:T(8,128)(2,1)} fusion(bf16[5120,512]{1,0:T(8,128)(2,1)} %get-tuple-element.167, s32[4096]{0:T(1024)S(1)} %fusion.37), kind=kCustom, calls=%fused_computation.1.clone.clone.1 | custom fusion | bytes 8404992 | tf_op jit(solution)/shard_map/while/body/eval_jaxpr/gather | solution.py:72
  455.4 18.1 %scatter_fusion.1 = f32[24,128,512]{2,1,0:T(8,128)} fusion(f32[24,128,512]{2,1,0:T(8,128)} %get-tuple-element.155, s32[32]{0:T(128)S(1)} %get-tuple-element.143, f32[32,128,512]{2,1,0:T(8,128)} %fusion.39), kind=kCustom, calls=%fused_computation.3.clone.clone.1 | custom fusion | flops 2097152 | bytes 25165952 | tf_op jit(solution)/shard_map/while/body/eval_jaxpr/scatter-add | solution.py:81
  473.5 20.6 %gather_fusion = bf16[4096,512]{1,0:T(8,128)(2,1)} fusion(bf16[5120,512]{1,0:T(8,128)(2,1)} %get-tuple-element.165, s32[4096]{0:T(1024)S(1)} %fusion.37), kind=kCustom, calls=%fused_computation.clone.clone.1 | custom fusion | bytes 8404992 | tf_op jit(solution)/shard_map/while/body/eval_jaxpr/gather | solution.py:71
  494.1 7.0 fusion.38
  501.1 18.2 %scatter_fusion = f32[24,512,128]{2,1,0:T(8,128)} fusion(f32[24,512,128]{2,1,0:T(8,128)} %get-tuple-element.154, s32[32]{0:T(128)S(1)} %get-tuple-element.143, f32[32,512,128]{2,1,0:T(8,128)} %fusion.38), kind=kCustom, calls=%fused_computation.2.clone.clone.1 | custom fusion | flops 2097152 | bytes 25165952 | tf_op jit(solution)/shard_map/while/body/eval_jaxpr/scatter-add | solution.py:81
  520.0 66.1 %reduce-scatter.5.cloned.1.call-done = f32[24,128,128]{2,1,0:T(8,128)} async-done(((f32[24,128,512]{2,1,0:T(8,128)}), f32[24,128,128]{2,1,0:T(8,128)}) %reduce-scatter.5.cloned.1.call-update) | async-done | bytes 1572880 | tf_op jit(solution)/shard_map/reduce_scatter | solution.py:92
  589.6 7.7 all-to-all-start.3
  597.2 57.7 %reduce-scatter.3.cloned.1.call-done = f32[24,128,128]{2,1,0:T(8,128)} async-done(((f32[24,512,128]{2,1,0:T(8,128)}), f32[24,128,128]{2,1,0:T(8,128)}) %reduce-scatter.3.cloned.1.call-update) | async-done | bytes 1572880 | tf_op jit(solution)/shard_map/reduce_scatter | solution.py:91
  657.3 47.2 %all_to_all.47 = f32[24,1,16,8,128]{4,0,3,1,2:T(8,128)S(1)} all-to-all(f32[24,1,16,8,128]{4,0,3,1,2:T(8,128)S(1)} %bitcast.69), channel_id=1, replica_groups=mesh['row'=4,'col'=16,'layer'=4] {'col'}, dimensions={2} | all-to-all | bytes 3145728 | tf_op jit(solution)/shard_map/all_to_all | solution.py:101
  704.5 27.5 %all_to_all.48 = f32[24,16,8,128]{3,0,2,1:T(8,128)S(1)} all-to-all(f32[24,16,8,128]{3,0,2,1:T(8,128)S(1)} %bitcast.68), channel_id=1, replica_groups=mesh['row'=4,'col'=16,'layer'=4] {'row','layer'}, dimensions={1} | all-to-all | bytes 3145728 | tf_op jit(solution)/shard_map/all_to_all | solution.py:105
  733.5 72.8 %psum.7 = f32[24,24]{1,0:T(8,128)} all-reduce(f32[24,24]{1,0:T(8,128)S(1)} %fusion.16), channel_id=1, replica_groups=mesh['row'=4,'col'=16,'layer'=4] {'row','col','layer'}, use_global_device_ids=true, to_apply=%region_10.11 | all-reduce | flops 576 | bytes 4608 | tf_op jit(solution)/shard_map/psum | solution.py:115
  (41 shorter events, 46.5 us)
Async XLA Ops:
  11.0 31.5 %all-to-all-start = ((s32[64,2,2]{1,2,0:T(2,128)}), s32[64,2,2]{1,2,0:T(2,128)S(1)}, u32[]{:S(2)}, u32[]{:S(2)}) async-start(s32[64,2,2]{1,2,0:T(2,128)} %copy.19), calls=%async_computation | async-start | bytes 131072 | tf_op jit(solution)/shard_map/all_to_all | solution.py:52
  42.4 103.9 %all-to-all-start.1 = ((bf16[128,128,128]{2,1,0:T(8,128)(2,1)}), bf16[128,128,128]{2,1,0:T(8,128)(2,1)}, u32[]{:S(2)}, u32[]{:S(2)}) async-start(bf16[128,128,128]{2,1,0:T(8,128)(2,1)} %scatter_fusion.2), calls=%async_computation.1 | async-start | bytes 8388608 | tf_op jit(solution)/shard_map/all_to_all | solution.py:45
  52.9 533.3 %reduce-scatter.5.cloned.1.call-start = ((), (), s32[]{:S(2)}) async-start(), calls=%async_computation.8 | async-start | bytes 7864320 | tf_op jit(solution)/shard_map/reduce_scatter | solution.py:92
  519.3 135.7 %reduce-scatter.3.cloned.1.call-start = ((), (), s32[]{:S(2)}) async-start(), calls=%async_computation.7 | async-start | bytes 7864320 | tf_op jit(solution)/shard_map/reduce_scatter | solution.py:91
  589.6 67.7 %all-to-all-start.3 = ((f32[24,1,16,8,128]{4,0,3,1,2:T(8,128)}), f32[24,1,16,8,128]{4,0,3,1,2:T(8,128)S(1)}, u32[]{:S(2)}, u32[]{:S(2)}) async-start(f32[24,1,16,8,128]{4,0,3,1,2:T(8,128)} %bitcast.6), calls=%async_computation.5 | async-start | bytes 3145728 | tf_op jit(solution)/shard_map/all_to_all | solution.py:102
Sparse Core Ops, SparseCore 0:
  519.4 66.6 reduce-scatter.4
  588.7 66.2 reduce-scatter.2
where the time goes:
time: 815 us; the launch traced here: 813 us
  waiting for transfers between devices  218 us (27%)
  local copies, waits for them, and re-layouts  195 us (24%)
  other arithmetic  151 us (19%)
  blocking collectives  147 us (18%)
  matrix products  57.5 us (7%)
  starting transfers between devices  31.3 us (4%)
  between operations  13.5 us (2%)
    all_to_all x1, waiting for transfers between devices, on_device(): lax.all_to_all(send_tiles.reshape(total_slots, tile_side, tile_side), ('c...  93.4 us
    gather x4, local copies, waits for them, and re-layouts, add_group(): virt_rows = virt_cols[row_index]  82.3 us
    gather x4, local copies, waits for them, and re-layouts, add_group(): occ_rows = occ_cols[row_index]  82.3 us
    psum x1, blocking collectives, on_device(): return lax.psum(chi_part, ('row', 'col', 'layer'))  72.8 us
    scatter-add x4, other arithmetic, add_group(): virt_total.at[aux_index].add(virt_term)  72.6 us
    scatter-add x4, other arithmetic, add_group(): occ_total.at[aux_index].add(occ_term)  72.5 us
    reduce_scatter x1, waiting for transfers between devices, on_device(): lax.psum_scatter(virt_total, 'layer', scatter_dimension=2, tiled=True)  66.1 us
    reduce_scatter x1, waiting for transfers between devices, on_device(): lax.psum_scatter(occ_total, 'layer', scatter_dimension=1, tiled=True)  57.7 us
  transfers between devices with their start and end apart: 5, of which 3 were waited for; matrix products, arithmetic and copies ran while one was open for 3% of the time, Pallas kernels for 0%

commit v1 on v0

--- a/solution.py
+++ b/solution.py
@@ -102,7 +102,18 @@
         lax.all_to_all(virt_five, "col", split_axis=2, concat_axis=1, tiled=True),
     )
     virt_four = virt_moved.reshape(aux_count, mesh_count, thin_rows, narrow)
-    virt_back = lax.all_to_all(virt_four, ("row", "layer"), split_axis=1, concat_axis=3, tiled=True)
+    ways, here = (lax.axis_size(("row", "layer")), lax.axis_index(("row", "layer")))
+    width = virt_four.shape[1] // ways
+    shape = list(virt_four.shape)
+    shape[1] = width
+    height = shape[3]
+    shape[3] = height * ways
+    virt_back = jnp.zeros(shape, virt_four.dtype)
+    for mask in range(ways):
+        part = lax.dynamic_slice_in_dim(virt_four, (here ^ mask) * width, width, axis=1)
+        if mask:
+            part = lax.ppermute(part, ("row", "layer"), [(d, d ^ mask) for d in range(ways)])
+        virt_back = lax.dynamic_update_slice_in_dim(virt_back, part, (here ^ mask) * height, axis=3)
     occ_final = occ_moved.reshape(aux_count, col_count, thin_rows, tile_side)
     virt_final = virt_back.reshape(aux_count, thin_rows, col_count, tile_side)
     chi_part = jnp.einsum(

time: 815 us -> 792 us (0.972)
  blocking collectives: 147 us -> 75.4 us
  starting transfers between devices: 31.3 us -> 67.2 us
  waiting for transfers between devices: 218 us -> 227 us
    all_to_all x2 -> x0, blocking collectives: 74.7 us -> none  [the longest x1 47.2 us: on_device(): lax.all_to_all(occ_five, 'col', split_axis=2, concat_axis=1, tiled=True)]
    ppermute x0 -> x15, starting transfers between devices: none -> 28.2 us  [on_device(): lax.ppermute(part, ('row', 'layer'), [(d, d ^ mask) for d in range(ways)])]
  transfers between devices with their start and end apart: 5 -> 21, of which waited for: 3 -> 6; matrix products, arithmetic and copies ran while one was open for 3% -> 3% of each run, Pallas kernels for 0% -> 0%
where the time goes in v1:
time: 792 us; the launch traced here: 790 us
  waiting for transfers between devices  227 us (29%)
  local copies, waits for them, and re-layouts  197 us (25%)
  other arithmetic  151 us (19%)
  blocking collectives  75.4 us (10%)
  starting transfers between devices  67.2 us (8%)
  matrix products  58.5 us (7%)
  between operations  13.7 us (2%)
    all_to_all x1, waiting for transfers between devices, on_device(): lax.all_to_all(send_tiles.reshape(total_slots, tile_side, tile_side), ('c...  93.4 us
    gather x4, local copies, waits for them, and re-layouts, add_group(): virt_rows = virt_cols[row_index]  82.6 us
    gather x4, local copies, waits for them, and re-layouts, add_group(): occ_rows = occ_cols[row_index]  82.6 us
    psum x1, blocking collectives, on_device(): return lax.psum(chi_part, ('row', 'col', 'layer'))  75.4 us
    scatter-add x4, other arithmetic, add_group(): virt_total.at[aux_index].add(virt_term)  72.9 us
    scatter-add x4, other arithmetic, add_group(): occ_total.at[aux_index].add(occ_term)  72.5 us
    reduce_scatter x1, waiting for transfers between devices, on_device(): lax.psum_scatter(virt_total, 'layer', scatter_dimension=2, tiled=True)  65.9 us
    reduce_scatter x1, waiting for transfers between devices, on_device(): lax.psum_scatter(occ_total, 'layer', scatter_dimension=1, tiled=True)  58.3 us
  transfers between devices with their start and end apart: 21, of which 6 were waited for; matrix products, arithmetic and copies ran while one was open for 3% of the time, Pallas kernels for 0%

profile of v1, /device:TPU:1, one launch (start us, length us, event | category | flops | bytes accessed | tf_op | source)
XLA Modules:
  0.0 790.0 jit_solution(3229699630187155139)
XLA Ops:
  11.0 13.0 %all-to-all-start = ((s32[64,2,2]{1,2,0:T(2,128)}), s32[64,2,2]{1,2,0:T(2,128)S(1)}, u32[]{:S(2)}, u32[]{:S(2)}) async-start(s32[64,2,2]{1,2,0:T(2,128)} %copy.25), calls=%async_computation | async-start | bytes 131072 | tf_op jit(solution)/shard_map/all_to_all | solution.py:52
  29.7 12.8 %scatter_fusion.2 = bf16[128,128,128]{2,1,0:T(8,128)(2,1)} fusion(bf16[128,128,128]{2,1,0:T(8,128)(2,1)} %broadcast_in_dim.44, s32[88]{0:T(128)S(1)} %compare_select_fusion.2, bf16[88,128,128]{2,1,0:T(8,128)(2,1)S(1)} %broadcast_select_fusion), kind=kCustom, calls=%fused_computation.5 | custom fusion | bytes 8651104 | tf_op jit(solution)/shard_map/scatter | solution.py:34
  42.5 10.4 %all-to-all-start.1 = ((bf16[128,128,128]{2,1,0:T(8,128)(2,1)}), bf16[128,128,128]{2,1,0:T(8,128)(2,1)}, u32[]{:S(2)}, u32[]{:S(2)}) async-start(bf16[128,128,128]{2,1,0:T(8,128)(2,1)} %scatter_fusion.2), calls=%async_computation.1 | async-start | bytes 8388608 | tf_op jit(solution)/shard_map/all_to_all | solution.py:45
  53.1 93.4 %all-to-all-done.1 = bf16[128,128,128]{2,1,0:T(8,128)(2,1)} async-done(((bf16[128,128,128]{2,1,0:T(8,128)(2,1)}), bf16[128,128,128]{2,1,0:T(8,128)(2,1)}, u32[]{:S(2)}, u32[]{:S(2)}) %all-to-all-start.1) | async-done | bytes 4194336 | tf_op jit(solution)/shard_map/all_to_all | solution.py:45
  153.2 367.0 %while.13 = (s32[]{:T(128)}, f32[24,512,128]{2,1,0:T(8,128)}, f32[24,128,512]{2,1,0:T(8,128)}, s32[4,32,2]{1,0,2:T(4,128)S(1)}, bf16[5120,512]{1,0:T(8,128)(2,1)...) while((s32[]{:T(128)}, f32[24,512,128]{2,1,0:T(8,128)}, ...), condition=%wide.region_7.8_spmd.clone, body=%wide.region_4.7_spmd.clone.sunk | while | flops 1077956736 | bytes 94423512 | solution.py:89
  153.3 20.6 %gather_fusion.1 = bf16[4096,512]{1,0:T(8,128)(2,1)} fusion(bf16[5120,512]{1,0:T(8,128)(2,1)} %get-tuple-element.189, s32[4096]{0:T(1024)S(1)} %fusion.37), kind=kCustom, calls=%fused_computation.1.clone.clone.1 | custom fusion | bytes 8404992 | tf_op jit(solution)/shard_map/while/body/eval_jaxpr/gather | solution.py:72
  181.0 18.1 %scatter_fusion.1 = f32[24,128,512]{2,1,0:T(8,128)} fusion(f32[24,128,512]{2,1,0:T(8,128)} %get-tuple-element.177, s32[32]{0:T(128)S(1)} %get-tuple-element.165, f32[32,128,512]{2,1,0:T(8,128)} %fusion.39), kind=kCustom, calls=%fused_computation.3.clone.clone.1 | custom fusion | flops 2097152 | bytes 25165952 | tf_op jit(solution)/shard_map/while/body/eval_jaxpr/scatter-add | solution.py:81
  199.0 20.6 %gather_fusion = bf16[4096,512]{1,0:T(8,128)(2,1)} fusion(bf16[5120,512]{1,0:T(8,128)(2,1)} %get-tuple-element.187, s32[4096]{0:T(1024)S(1)} %fusion.37), kind=kCustom, calls=%fused_computation.clone.clone.1 | custom fusion | bytes 8404992 | tf_op jit(solution)/shard_map/while/body/eval_jaxpr/gather | solution.py:71
  219.7 7.0 fusion.38
  226.7 18.1 %scatter_fusion = f32[24,512,128]{2,1,0:T(8,128)} fusion(f32[24,512,128]{2,1,0:T(8,128)} %get-tuple-element.176, s32[32]{0:T(128)S(1)} %get-tuple-element.165, f32[32,512,128]{2,1,0:T(8,128)} %fusion.38), kind=kCustom, calls=%fused_computation.2.clone.clone.1 | custom fusion | flops 2097152 | bytes 25165952 | tf_op jit(solution)/shard_map/while/body/eval_jaxpr/scatter-add | solution.py:81
  244.9 20.6 %gather_fusion.1 = bf16[4096,512]{1,0:T(8,128)(2,1)} fusion(bf16[5120,512]{1,0:T(8,128)(2,1)} %get-tuple-element.189, s32[4096]{0:T(1024)S(1)} %fusion.37), kind=kCustom, calls=%fused_computation.1.clone.clone.1 | custom fusion | bytes 8404992 | tf_op jit(solution)/shard_map/while/body/eval_jaxpr/gather | solution.py:72
  265.5 7.0 fusion.39
  272.5 18.2 %scatter_fusion.1 = f32[24,128,512]{2,1,0:T(8,128)} fusion(f32[24,128,512]{2,1,0:T(8,128)} %get-tuple-element.177, s32[32]{0:T(128)S(1)} %get-tuple-element.165, f32[32,128,512]{2,1,0:T(8,128)} %fusion.39), kind=kCustom, calls=%fused_computation.3.clone.clone.1 | custom fusion | flops 2097152 | bytes 25165952 | tf_op jit(solution)/shard_map/while/body/eval_jaxpr/scatter-add | solution.py:81
  290.7 20.6 %gather_fusion = bf16[4096,512]{1,0:T(8,128)(2,1)} fusion(bf16[5120,512]{1,0:T(8,128)(2,1)} %get-tuple-element.187, s32[4096]{0:T(1024)S(1)} %fusion.37), kind=kCustom, calls=%fused_computation.clone.clone.1 | custom fusion | bytes 8404992 | tf_op jit(solution)/shard_map/while/body/eval_jaxpr/gather | solution.py:71
  311.4 7.0 fusion.38
  318.4 18.0 %scatter_fusion = f32[24,512,128]{2,1,0:T(8,128)} fusion(f32[24,512,128]{2,1,0:T(8,128)} %get-tuple-element.176, s32[32]{0:T(128)S(1)} %get-tuple-element.165, f32[32,512,128]{2,1,0:T(8,128)} %fusion.38), kind=kCustom, calls=%fused_computation.2.clone.clone.1 | custom fusion | flops 2097152 | bytes 25165952 | tf_op jit(solution)/shard_map/while/body/eval_jaxpr/scatter-add | solution.py:81
  336.5 20.6 %gather_fusion.1 = bf16[4096,512]{1,0:T(8,128)(2,1)} fusion(bf16[5120,512]{1,0:T(8,128)(2,1)} %get-tuple-element.189, s32[4096]{0:T(1024)S(1)} %fusion.37), kind=kCustom, calls=%fused_computation.1.clone.clone.1 | custom fusion | bytes 8404992 | tf_op jit(solution)/shard_map/while/body/eval_jaxpr/gather | solution.py:72
  364.2 18.4 %scatter_fusion.1 = f32[24,128,512]{2,1,0:T(8,128)} fusion(f32[24,128,512]{2,1,0:T(8,128)} %get-tuple-element.177, s32[32]{0:T(128)S(1)} %get-tuple-element.165, f32[32,128,512]{2,1,0:T(8,128)} %fusion.39), kind=kCustom, calls=%fused_computation.3.clone.clone.1 | custom fusion | flops 2097152 | bytes 25165952 | tf_op jit(solution)/shard_map/while/body/eval_jaxpr/scatter-add | solution.py:81
  382.5 20.6 %gather_fusion = bf16[4096,512]{1,0:T(8,128)(2,1)} fusion(bf16[5120,512]{1,0:T(8,128)(2,1)} %get-tuple-element.187, s32[4096]{0:T(1024)S(1)} %fusion.37), kind=kCustom, calls=%fused_computation.clone.clone.1 | custom fusion | bytes 8404992 | tf_op jit(solution)/shard_map/while/body/eval_jaxpr/gather | solution.py:71
  403.2 7.0 fusion.38
  410.2 18.3 %scatter_fusion = f32[24,512,128]{2,1,0:T(8,128)} fusion(f32[24,512,128]{2,1,0:T(8,128)} %get-tuple-element.176, s32[32]{0:T(128)S(1)} %get-tuple-element.165, f32[32,512,128]{2,1,0:T(8,128)} %fusion.38), kind=kCustom, calls=%fused_computation.2.clone.clone.1 | custom fusion | flops 2097152 | bytes 25165952 | tf_op jit(solution)/shard_map/while/body/eval_jaxpr/scatter-add | solution.py:81
  428.6 20.6 %gather_fusion.1 = bf16[4096,512]{1,0:T(8,128)(2,1)} fusion(bf16[5120,512]{1,0:T(8,128)(2,1)} %get-tuple-element.189, s32[4096]{0:T(1024)S(1)} %fusion.37), kind=kCustom, calls=%fused_computation.1.clone.clone.1 | custom fusion | bytes 8404992 | tf_op jit(solution)/shard_map/while/body/eval_jaxpr/gather | solution.py:72
  449.3 7.0 fusion.39
  456.2 18.2 %scatter_fusion.1 = f32[24,128,512]{2,1,0:T(8,128)} fusion(f32[24,128,512]{2,1,0:T(8,128)} %get-tuple-element.177, s32[32]{0:T(128)S(1)} %get-tuple-element.165, f32[32,128,512]{2,1,0:T(8,128)} %fusion.39), kind=kCustom, calls=%fused_computation.3.clone.clone.1 | custom fusion | flops 2097152 | bytes 25165952 | tf_op jit(solution)/shard_map/while/body/eval_jaxpr/scatter-add | solution.py:81
  474.4 20.6 %gather_fusion = bf16[4096,512]{1,0:T(8,128)(2,1)} fusion(bf16[5120,512]{1,0:T(8,128)(2,1)} %get-tuple-element.187, s32[4096]{0:T(1024)S(1)} %fusion.37), kind=kCustom, calls=%fused_computation.clone.clone.1 | custom fusion | bytes 8404992 | tf_op jit(solution)/shard_map/while/body/eval_jaxpr/gather | solution.py:71
  495.1 7.0 fusion.38
  502.1 18.1 %scatter_fusion = f32[24,512,128]{2,1,0:T(8,128)} fusion(f32[24,512,128]{2,1,0:T(8,128)} %get-tuple-element.176, s32[32]{0:T(128)S(1)} %get-tuple-element.165, f32[32,512,128]{2,1,0:T(8,128)} %fusion.38), kind=kCustom, calls=%fused_computation.2.clone.clone.1 | custom fusion | flops 2097152 | bytes 25165952 | tf_op jit(solution)/shard_map/while/body/eval_jaxpr/scatter-add | solution.py:81
  521.0 65.9 %reduce-scatter.5.cloned.1.call-done = f32[24,128,128]{2,1,0:T(8,128)} async-done(((f32[24,128,512]{2,1,0:T(8,128)}), f32[24,128,128]{2,1,0:T(8,128)}) %reduce-scatter.5.cloned.1.call-update) | async-done | bytes 1572880 | tf_op jit(solution)/shard_map/reduce_scatter | solution.py:92
  589.6 7.8 all-to-all-start.3
  597.5 58.3 %reduce-scatter.3.cloned.1.call-done = f32[24,128,128]{2,1,0:T(8,128)} async-done(((f32[24,512,128]{2,1,0:T(8,128)}), f32[24,128,128]{2,1,0:T(8,128)}) %reduce-scatter.3.cloned.1.call-update) | async-done | bytes 1572880 | tf_op jit(solution)/shard_map/reduce_scatter | solution.py:91
  659.2 7.6 all-to-all-start.2
  707.7 75.4 %psum.7 = f32[24,24]{1,0:T(8,128)} all-reduce(f32[24,24]{1,0:T(8,128)S(1)} %fusion.16), channel_id=1, replica_groups=mesh['row'=4,'col'=16,'layer'=4] {'row','col','layer'}, use_global_device_ids=true, to_apply=%region_10.11 | all-reduce | flops 576 | bytes 4608 | tf_op jit(solution)/shard_map/psum | solution.py:126
  (90 shorter events, 78.9 us)
Async XLA Ops:
  11.0 31.6 %all-to-all-start = ((s32[64,2,2]{1,2,0:T(2,128)}), s32[64,2,2]{1,2,0:T(2,128)S(1)}, u32[]{:S(2)}, u32[]{:S(2)}) async-start(s32[64,2,2]{1,2,0:T(2,128)} %copy.25), calls=%async_computation | async-start | bytes 131072 | tf_op jit(solution)/shard_map/all_to_all | solution.py:52
  42.5 103.9 %all-to-all-start.1 = ((bf16[128,128,128]{2,1,0:T(8,128)(2,1)}), bf16[128,128,128]{2,1,0:T(8,128)(2,1)}, u32[]{:S(2)}, u32[]{:S(2)}) async-start(bf16[128,128,128]{2,1,0:T(8,128)(2,1)} %scatter_fusion.2), calls=%async_computation.1 | async-start | bytes 8388608 | tf_op jit(solution)/shard_map/all_to_all | solution.py:45
  53.0 534.0 %reduce-scatter.5.cloned.1.call-start = ((), (), s32[]{:S(2)}) async-start(), calls=%async_computation.7 | async-start | bytes 7864320 | tf_op jit(solution)/shard_map/reduce_scatter | solution.py:92
  520.3 135.5 %reduce-scatter.3.cloned.1.call-start = ((), (), s32[]{:S(2)}) async-start(), calls=%async_computation.6 | async-start | bytes 7864320 | tf_op jit(solution)/shard_map/reduce_scatter | solution.py:91
  589.6 69.6 %all-to-all-start.3 = ((f32[24,1,16,8,128]{4,3,0,1,2:T(8,128)}), f32[24,1,16,8,128]{4,3,0,1,2:T(8,128)S(1)}, u32[]{:S(2)}, u32[]{:S(2)}) async-start(f32[24,1,16,8,128]{4,3,0,1,2:T(8,128)} %copy.29), calls=%async_computation.5 | async-start | bytes 3145728 | tf_op jit(solution)/shard_map/all_to_all | solution.py:102
  659.2 46.1 %all-to-all-start.2 = ((f32[24,1,16,8,128]{4,0,3,1,2:T(8,128)}), f32[24,1,16,8,128]{4,0,3,1,2:T(8,128)S(1)}, u32[]{:S(2)}, u32[]{:S(2)}) async-start(f32[24,1,16,8,128]{4,0,3,1,2:T(8,128)} %bitcast.4), calls=%async_computation.3 | async-start | bytes 3145728 | tf_op jit(solution)/shard_map/all_to_all | solution.py:101
  667.0 5.4 collective-permute-start
  667.1 8.1 %collective-permute-start.1 = (f32[24,1,8,128]{3,2,0,1:T(8,128)S(1)}, f32[24,1,8,128]{3,2,0,1:T(8,128)S(1)}, u32[]{:S(2)}, u32[]{:S(2)}) collective-permute-start(f32[24,1,8,128]{3,2,0,1:T(8,128)S(1)} %get-tuple-element.118), channel_id=1, source_target_pairs={{0,2},{1,3},{2,0},{3,1},{64,66},{65,67},{66,64},{67,65},{128,130},... | collective-permute-start | bytes 294920 | tf_op jit(solution)/shard_map/ppermute | solution.py:115
  668.9 8.4 %collective-permute-start.2 = (f32[24,1,8,128]{3,2,0,1:T(8,128)S(1)}, f32[24,1,8,128]{3,2,0,1:T(8,128)S(1)}, u32[]{:S(2)}, u32[]{:S(2)}) collective-permute-start(f32[24,1,8,128]{3,2,0,1:T(8,128)S(1)} %get-tuple-element.117), channel_id=1, source_target_pairs={{0,3},{1,2},{2,1},{3,0},{64,67},{65,66},{66,65},{67,64},{128,131},... | collective-permute-start | bytes 294920 | tf_op jit(solution)/shard_map/ppermute | solution.py:115
  671.0 9.2 %collective-permute-start.3 = (f32[24,1,8,128]{3,2,0,1:T(8,128)S(1)}, f32[24,1,8,128]{3,2,0,1:T(8,128)S(1)}, u32[]{:S(2)}, u32[]{:S(2)}) collective-permute-start(f32[24,1,8,128]{3,2,0,1:T(8,128)S(1)} %get-tuple-element.116), channel_id=1, source_target_pairs={{0,64},{1,65},{2,66},{3,67},{64,0},{65,1},{66,2},{67,3},{128,192},... | collective-permute-start | bytes 294920 | tf_op jit(solution)/shard_map/ppermute | solution.py:115
  672.2 8.1 %collective-permute-start.4 = (f32[24,1,8,128]{3,2,0,1:T(8,128)S(1)}, f32[24,1,8,128]{3,2,0,1:T(8,128)S(1)}, u32[]{:S(2)}, u32[]{:S(2)}) collective-permute-start(f32[24,1,8,128]{3,2,0,1:T(8,128)S(1)} %get-tuple-element.115), channel_id=1, source_target_pairs={{0,65},{1,64},{2,67},{3,66},{64,1},{65,0},{66,3},{67,2},{128,193},... | collective-permute-start | bytes 294920 | tf_op jit(solution)/shard_map/ppermute | solution.py:115
  672.4 12.4 %collective-permute-start.5 = (f32[24,1,8,128]{3,2,0,1:T(8,128)S(1)}, f32[24,1,8,128]{3,2,0,1:T(8,128)S(1)}, u32[]{:S(2)}, u32[]{:S(2)}) collective-permute-start(f32[24,1,8,128]{3,2,0,1:T(8,128)S(1)} %get-tuple-element.114), channel_id=1, source_target_pairs={{0,66},{1,67},{2,64},{3,65},{64,2},{65,3},{66,0},{67,1},{128,194},... | collective-permute-start | bytes 294920 | tf_op jit(solution)/shard_map/ppermute | solution.py:115
  675.2 11.5 %collective-permute-start.6 = (f32[24,1,8,128]{3,2,0,1:T(8,128)S(1)}, f32[24,1,8,128]{3,2,0,1:T(8,128)S(1)}, u32[]{:S(2)}, u32[]{:S(2)}) collective-permute-start(f32[24,1,8,128]{3,2,0,1:T(8,128)S(1)} %get-tuple-element.113), channel_id=1, source_target_pairs={{0,67},{1,66},{2,65},{3,64},{64,3},{65,2},{66,1},{67,0},{128,195},... | collective-permute-start | bytes 294920 | tf_op jit(solution)/shard_map/ppermute | solution.py:115
  677.3 12.0 %collective-permute-start.7 = (f32[24,1,8,128]{3,2,0,1:T(8,128)S(1)}, f32[24,1,8,128]{3,2,0,1:T(8,128)S(1)}, u32[]{:S(2)}, u32[]{:S(2)}) collective-permute-start(f32[24,1,8,128]{3,2,0,1:T(8,128)S(1)} %get-tuple-element.112), channel_id=1, source_target_pairs={{0,128},{1,129},{2,130},{3,131},{64,192},{65,193},{66,194},{67,195... | collective-permute-start | bytes 294920 | tf_op jit(solution)/shard_map/ppermute | solution.py:115
  680.2 9.3 %collective-permute-start.8 = (f32[24,1,8,128]{3,2,0,1:T(8,128)S(1)}, f32[24,1,8,128]{3,2,0,1:T(8,128)S(1)}, u32[]{:S(2)}, u32[]{:S(2)}) collective-permute-start(f32[24,1,8,128]{3,2,0,1:T(8,128)S(1)} %get-tuple-element.111), channel_id=1, source_target_pairs={{0,129},{1,128},{2,131},{3,130},{64,193},{65,192},{66,195},{67,194... | collective-permute-start | bytes 294920 | tf_op jit(solution)/shard_map/ppermute | solution.py:115
  680.3 13.3 %collective-permute-start.9 = (f32[24,1,8,128]{3,2,0,1:T(8,128)S(1)}, f32[24,1,8,128]{3,2,0,1:T(8,128)S(1)}, u32[]{:S(2)}, u32[]{:S(2)}) collective-permute-start(f32[24,1,8,128]{3,2,0,1:T(8,128)S(1)} %get-tuple-element.110), channel_id=1, source_target_pairs={{0,130},{1,131},{2,128},{3,129},{64,194},{65,195},{66,192},{67,193... | collective-permute-start | bytes 294920 | tf_op jit(solution)/shard_map/ppermute | solution.py:115
  684.8 11.0 %collective-permute-start.10 = (f32[24,1,8,128]{3,2,0,1:T(8,128)S(1)}, f32[24,1,8,128]{3,2,0,1:T(8,128)S(1)}, u32[]{:S(2)}, u32[]{:S(2)}) collective-permute-start(f32[24,1,8,128]{3,2,0,1:T(8,128)S(1)} %get-tuple-element.109), channel_id=1, source_target_pairs={{0,131},{1,130},{2,129},{3,128},{64,195},{65,194},{66,193},{67,192... | collective-permute-start | bytes 294920 | tf_op jit(solution)/shard_map/ppermute | solution.py:115
  686.7 9.1 %collective-permute-start.11 = (f32[24,1,8,128]{3,2,0,1:T(8,128)S(1)}, f32[24,1,8,128]{3,2,0,1:T(8,128)S(1)}, u32[]{:S(2)}, u32[]{:S(2)}) collective-permute-start(f32[24,1,8,128]{3,2,0,1:T(8,128)S(1)} %get-tuple-element.108), channel_id=1, source_target_pairs={{0,192},{1,193},{2,194},{3,195},{64,128},{65,129},{66,130},{67,131... | collective-permute-start | bytes 294920 | tf_op jit(solution)/shard_map/ppermute | solution.py:115
  689.3 6.5 collective-permute-start.12
  689.4 7.9 %collective-permute-start.13 = (f32[24,1,8,128]{3,2,0,1:T(8,128)S(1)}, f32[24,1,8,128]{3,2,0,1:T(8,128)S(1)}, u32[]{:S(2)}, u32[]{:S(2)}) collective-permute-start(f32[24,1,8,128]{3,2,0,1:T(8,128)S(1)} %get-tuple-element.106), channel_id=1, source_target_pairs={{0,194},{1,195},{2,192},{3,193},{64,130},{65,131},{66,128},{67,129... | collective-permute-start | bytes 294920 | tf_op jit(solution)/shard_map/ppermute | solution.py:115
  693.6 8.4 %collective-permute-start.14 = (f32[24,1,8,128]{3,2,0,1:T(8,128)S(1)}, f32[24,1,8,128]{3,2,0,1:T(8,128)S(1)}, u32[]{:S(2)}, u32[]{:S(2)}) collective-permute-start(f32[24,1,8,128]{3,2,0,1:T(8,128)S(1)} %get-tuple-element.105), channel_id=1, source_target_pairs={{0,195},{1,194},{2,193},{3,192},{64,131},{65,130},{66,129},{67,128... | collective-permute-start | bytes 294920 | tf_op jit(solution)/shard_map/ppermute | solution.py:115
Sparse Core Ops, SparseCore 0:
  520.4 66.4 reduce-scatter.4
  589.5 66.2 reduce-scatter.2
